TPU v7x, 32 devices: a whole 2x2x4 slice. The times are simulated.
32 devices in a mesh: ctx: 8 (over z, core), tp: 4 (over y, x).
Axes of the slice: x: 2, y: 2, z: 4, core: 2. Of those that a mesh axis runs over, the one named last changes fastest.
Arguments:
- tokens: bfloat16 [4096, 4096], P(('ctx', 'tp')), may hold values from -6 to 6
- in_weight: bfloat16 [3, 4096, 2048], P(None, None, 'tp'), may hold values from -0.09375 to 0.09375
- short_taps: float32 [3, 3, 2048], P(None, None, 'tp'), may hold values from -3 to 3
- decay_rate: float32 [16, 2048], P(None, 'tp'), may hold values from 4.8828125e-05 to 0.0333333333
- residue: float32 [16, 2048], P(None, 'tp'), may hold values from -0.26 to 0.26
- skip_gain: float32 [2048], P('tp'), may hold values from -4 to 4
- grad_out: bfloat16 [4096, 2048], P('ctx', 'tp'), may hold values from -6 to 6
Outputs:
- mixed_out: bfloat16 [4096, 2048], P('ctx', 'tp')
- input_grad: bfloat16 [4096, 4096], P(('ctx', 'tp'))
All inputs are finite; a program needn't handle non-finite values.
Results may differ from a plain program's by a relative error of at most 0.0065.
Values may be sent and summed in bfloat16 or wider, within the bound.
A program may use at most 192 MiB of HBM per device.

v0:
```python
import jax
import jax.numpy as jnp
from jax import lax
from jax.sharding import PartitionSpec as P

exact_mode = lax.Precision.HIGHEST


def from_behind(value, axis, steps):
    count = lax.axis_size(axis)
    leading, last = (max(0, -steps), min(count, count - steps))
    return lax.ppermute(value, axis, [(source, source + steps) for source in range(leading, last)])


def modal_block(signal, log_pole, residue):
    length, channels = signal.shape
    sub_len = min(64, length)
    sub_count = length // sub_len
    offsets = jnp.arange(sub_len, dtype=jnp.float32)
    sections = signal.reshape(sub_count, sub_len, channels)
    powers = jnp.exp(log_pole[:, None, :] * offsets[None, :, None])
    filter_taps = jnp.sum(residue[:, None, :] * powers, axis=0)
    lag_index = jnp.arange(sub_len)[:, None] - jnp.arange(sub_len)[None, :]
    toeplitz = jnp.where((lag_index >= 0)[:, :, None], filter_taps[jnp.maximum(lag_index, 0)], 0.0)
    within = jnp.einsum("abc,kbc->kac", toeplitz, sections, precision=exact_mode)
    to_end = jnp.exp(log_pole[:, None, :] * (sub_len - 1.0 - offsets)[None, :, None])
    end_states = jnp.einsum("nbc,kbc->nkc", to_end, sections, precision=exact_mode)
    lag_blocks = jnp.arange(sub_count + 1)[:, None] - 1 - jnp.arange(sub_count)[None, :]
    valid_lag = lag_blocks >= 0
    lag_float = (jnp.maximum(lag_blocks, 0) * sub_len).astype(jnp.float32)
    decay_table = jnp.exp(log_pole[None, None] * lag_float[:, :, None, None])
    decay_table = jnp.where(valid_lag[:, :, None, None], decay_table, 0.0)
    carried = jnp.einsum("kmnc,nmc->nkc", decay_table, end_states, precision=exact_mode)
    stepped = residue[:, None, :] * jnp.exp(log_pole[:, None, :] * (offsets[None, :, None] + 1.0))
    output = within + jnp.einsum(
        "nac,nkc->kac", stepped, carried[:, :sub_count], precision=exact_mode
    )
    return (output.reshape(length, channels), carried[:, sub_count])


def carry_term(incoming, log_pole, residue, length):
    channels = incoming.shape[1]
    sub_len = min(64, length)
    sub_count = length // sub_len
    offsets = jnp.arange(sub_len, dtype=jnp.float32)
    stepped = residue[:, None, :] * jnp.exp(log_pole[:, None, :] * (offsets[None, :, None] + 1.0))
    block_starts = (jnp.arange(sub_count) * sub_len).astype(jnp.float32)
    start_states = incoming[:, None, :] * jnp.exp(
        log_pole[:, None, :] * block_starts[None, :, None]
    )
    output = jnp.einsum("nac,nkc->kac", stepped, start_states, precision=exact_mode)
    return output.reshape(length, channels)


def shards(tokens, in_weight, short_taps, decay_rate, residue, skip_gain, grad_out):
    width = in_weight.shape[2]
    weight_cat = jnp.concatenate([in_weight[0], in_weight[1], in_weight[2]], axis=1)
    streams = jnp.dot(
        lax.all_gather(tokens, "tp", axis=0, tiled=True),
        weight_cat,
        preferred_element_type=jnp.float32,
    ).astype(jnp.bfloat16)
    length = streams.shape[0]
    tap_reach = short_taps.shape[1] - 1
    taps_cat = jnp.concatenate([short_taps[0], short_taps[1], short_taps[2]], axis=1)
    before = from_behind(streams[length - tap_reach :], "ctx", 1)
    extended = jnp.concatenate([before, streams], axis=0).astype(jnp.float32)
    short_mixed = taps_cat[0][None] * extended[tap_reach:]
    for offset in range(1, tap_reach + 1):
        short_mixed = (
            short_mixed
            + taps_cat[offset][None] * extended[tap_reach - offset : tap_reach - offset + length]
        )
    query_side = short_mixed[:, :width]
    key_side = short_mixed[:, width : 2 * width]
    value_side = short_mixed[:, 2 * width :]
    product_in = key_side * value_side
    log_pole = -decay_rate
    forward_local, forward_sum = modal_block(product_in, log_pole, residue)
    upstream = grad_out.astype(jnp.float32)
    conv_grad = upstream * query_side
    backward_local, backward_sum = modal_block(conv_grad[::-1], log_pole, residue)
    position = lax.axis_index("ctx")
    summaries = (
        lax.all_gather(forward_sum[None], "ctx", axis=0, tiled=True),
        lax.all_gather(backward_sum[None], "ctx", axis=0, tiled=True),
    )
    block_index = jnp.arange(summaries[0].shape[0])
    earlier_gap = position - 1 - block_index
    later_gap = block_index - position - 1
    scale_fwd = (jnp.maximum(earlier_gap, 0) * length).astype(jnp.float32)
    scale_bwd = (jnp.maximum(later_gap, 0) * length).astype(jnp.float32)
    weight_fwd = jnp.where(
        (earlier_gap >= 0)[:, None, None], jnp.exp(log_pole[None] * scale_fwd[:, None, None]), 0.0
    )
    weight_bwd = jnp.where(
        (later_gap >= 0)[:, None, None], jnp.exp(log_pole[None] * scale_bwd[:, None, None]), 0.0
    )
    incoming_fwd = jnp.sum(weight_fwd * summaries[0], axis=0)
    incoming_bwd = jnp.sum(weight_bwd * summaries[1], axis=0)
    conv_out = forward_local + carry_term(incoming_fwd, log_pole, residue, length)
    back_conv = (backward_local + carry_term(incoming_bwd, log_pole, residue, length))[::-1]
    filtered = conv_out + skip_gain[None] * product_in
    result = (query_side * filtered).astype(jnp.bfloat16)
    grad_query = upstream * filtered
    grad_product = back_conv + skip_gain[None] * conv_grad
    stream_grads = jnp.concatenate(
        [grad_query, grad_product * value_side, grad_product * key_side], axis=1
    )
    after_rows = from_behind(stream_grads[:tap_reach], "ctx", -1)
    padded = jnp.concatenate([stream_grads, after_rows], axis=0)
    grad_streams = taps_cat[0][None] * padded[:length]
    for offset in range(1, tap_reach + 1):
        grad_streams = grad_streams + taps_cat[offset][None] * padded[offset : offset + length]
    grad_streams = grad_streams.astype(jnp.bfloat16)
    input_grad = lax.psum_scatter(
        jnp.einsum("rk,dk->rd", grad_streams, weight_cat, preferred_element_type=jnp.float32),
        "tp",
        scatter_dimension=0,
        tiled=True,
    )
    return (result, input_grad.astype(jnp.bfloat16))


def solution(mesh):
    in_specs = (
        P(("ctx", "tp"), None),
        P(None, None, "tp"),
        P(None, None, "tp"),
        P(None, "tp"),
        P(None, "tp"),
        P("tp"),
        P("ctx", "tp"),
    )
    out_specs = (P("ctx", "tp"), P(("ctx", "tp"), None))
    return jax.shard_map(shards, mesh=mesh, in_specs=in_specs, out_specs=out_specs, check_vma=False)
```

profile of v0, /device:TPU:0, one launch (start us, length us, event | category | flops | bytes accessed | tf_op | source)
XLA Modules:
  0.0 425.8 jit_solution(13734944484443830677)
XLA Ops:
  7.2 0.7 all-gather.4.cloned.1.call-update
  7.9 0.8 neg.3
  8.9 0.9 copy.28
  10.1 0.7 slice_bitcast_fusion.5
  10.8 6.0 %multiply_reduce_fusion = f32[64,512]{0,1:T(8,128)S(1)} fusion(f32[16,512]{0,1:T(8,128)S(1)} %copy.29, f32[16,512]{0,1:T(8,128)S(1)} %copy.28), kind=kLoop, calls=%fused_computation.20 | loop fusion | flops 1540096 | bytes 196608 | tf_op jit(solution)/shard_map/reduce_sum | solution.py:22
  16.8 10.3 %slice_bitcast_fusion.2 = (bf16[4096,512]{1,0:T(8,128)(2,1)}, bf16[4096,512]{1,0:T(8,128)(2,1)}, bf16[4096,512]{1,0:T(8,128)(2,1)}) fusion(bf16[3,4096,512]{2,1,0:T(8,128)(2,1)} %param.8), kind=kLoop, calls=%fused_computation.23 | loop fusion | bytes 25165824 | tf_op jit(solution)/shard_map/squeeze | solution.py:57
  27.1 38.0 %all-gather.4.cloned.1.call-done = bf16[512,4096]{1,0:T(8,128)(2,1)} async-done(((bf16[128,4096]{1,0:T(8,128)(2,1)}), bf16[512,4096]{1,0:T(8,128)(2,1)}) %all-gather.4.cloned.1.call-update) | async-done | bytes 4194320 | tf_op jit(solution)/shard_map/all_gather | solution.py:59
  65.1 12.5 %fusion.22 = bf16[512,1536]{1,0:T(8,128)(2,1)S(1)} fusion(bf16[512,4096]{1,0:T(8,128)(2,1)} %all-gather.4.cloned.1.call-done, bf16[4096,512]{1,0:T(8,128)(2,1)} %get-tuple-element.10, bf16[4096,512]{1,0:T(8,128)(2,1)} %get-tuple-element.11, bf16[4096,512]{1,0:T(8,128)(2,1)} %get-tuple-element.9), kind=kOutput, calls=%fused_computation.37 | convolution fusion | flops 6480986112 | bytes 18350080 | tf_op jit(solution)/shard_map/dot_general | solution.py:58
  77.7 1.7 collective-permute-start
  79.5 16.8 %gather_fusion = f32[4096,512]{1,0:T(8,128)} fusion(f32[64,512]{1,0:T(8,128)S(1)} %copy.30, s32[4096]{0:T(1024)S(1)} %broadcast_clamp_fusion), kind=kCustom, calls=%fused_computation | custom fusion | bytes 16793600 | tf_op jit(solution)/shard_map/gather | solution.py:24
  96.4 16.3 %copy.31 = f32[64,64,512]{1,0,2:T(8,128)} copy(f32[64,64,512]{2,1,0:T(8,128)} %bitcast.51) | data formatting | bytes 16777216 | tf_op jit(solution)/shard_map/gather | solution.py:24
  113.2 0.9 fusion.19
  114.2 1.7 convert_multiply_fusion
  116.0 8.9 %rev.6 = f32[512,512]{1,0:T(8,128)} reverse(f32[512,512]{1,0:T(8,128)} %get-tuple-element.15), dimensions={0} | reverse | bytes 2097152 | tf_op jit(solution)/shard_map/rev | solution.py:82
  124.9 3.2 copy.38
  128.1 3.2 copy.32
  131.2 9.5 %fusion.43 = f32[16,512,8]{0,2,1:T(8,128)} fusion(f32[8,64,512]{1,0,2:T(8,128)} %copy.32, f32[64]{0:T(128)S(1)} %iota_subtract_fusion.2, f32[16,512]{0,1:T(8,128)S(1)} %copy.29), kind=kOutput, calls=%fused_computation.64 | convolution fusion | flops 50855936 | bytes 1343744 | tf_op jit(solution)/shard_map/nbc,kbc->nkc/dot_general | solution.py:27
  140.7 30.2 %fusion.2 = f32[512,8,64]{2,1,0:T(8,128)} fusion(f32[8,64,512]{1,0,2:T(8,128)S(1)} %copy-done.1, f32[64,64,512]{1,0,2:T(8,128)} %copy.31, pred[64,64]{1,0:T(8,128)(4,1)S(1)} %subtract_compare_fusion), kind=kOutput, calls=%fused_computation.3 | convolution fusion | flops 203423744 | bytes 10489856 | tf_op jit(solution)/shard_map/abc,kbc->kac/dot_general | solution.py:25
  170.9 30.5 %fusion = f32[512,8,64]{2,1,0:T(8,128)} fusion(f32[8,64,512]{1,0,2:T(8,128)S(1)} %copy-done, f32[64,64,512]{1,0,2:T(8,128)} %copy.31, pred[64,64]{1,0:T(8,128)(4,1)S(1)} %subtract_compare_fusion), kind=kOutput, calls=%fused_computation.1 | convolution fusion | flops 203423744 | bytes 10489856 | tf_op jit(solution)/shard_map/abc,kbc->kac/dot_general | solution.py:25
  201.4 8.3 %fusion.44 = f32[16,512,8]{0,2,1:T(8,128)} fusion(f32[8,64,512]{1,0,2:T(8,128)S(1)} %copy-done, f32[64]{0:T(128)S(1)} %iota_subtract_fusion.2, f32[16,512]{0,1:T(8,128)S(1)} %copy.29), kind=kOutput, calls=%fused_computation.65 | convolution fusion | flops 50855936 | bytes 1343744 | tf_op jit(solution)/shard_map/nbc,kbc->nkc/dot_general | solution.py:27
  209.7 2.9 copy.61
  212.6 2.9 copy.62
  215.4 2.8 multiply_reduce_fusion.1
  218.2 4.5 %copy.58 = f32[16,512,9]{0,2,1:T(8,128)} copy(f32[16,512,9]{1,0,2:T(8,128)} %get-tuple-element.2) | data formatting | bytes 589824 | tf_op jit(solution)/shard_map/kmnc,nmc->nkc/dot_general | solution.py:33
  222.7 2.4 slice.107
  225.1 1.0 copy.40
  226.2 14.7 %all-gather.1 = f32[128,1,512]{2,1,0:T(1,128)S(1)} all-gather(f32[16,1,512]{2,1,0:T(1,128)S(1)} %copy.40), channel_id=3, replica_groups=mesh['ctx'=8,'tp'=4] {'ctx'}, dimensions={0}, use_global_device_ids=true | all-gather | bytes 294912 | tf_op jit(solution)/shard_map/all_gather | solution.py:86
  240.9 0.7 copy.60
  241.6 4.5 %copy.50 = f32[16,512,9]{0,2,1:T(8,128)} copy(f32[16,512,9]{1,0,2:T(8,128)} %get-tuple-element.3) | data formatting | bytes 589824 | tf_op jit(solution)/shard_map/kmnc,nmc->nkc/dot_general | solution.py:33
  246.1 2.4 slice.105
  248.5 1.0 copy.34
  249.6 14.2 %all-gather = f32[128,1,512]{2,1,0:T(1,128)S(1)} all-gather(f32[16,1,512]{2,1,0:T(1,128)S(1)} %copy.34), channel_id=2, replica_groups=mesh['ctx'=8,'tp'=4] {'ctx'}, dimensions={0}, use_global_device_ids=true | all-gather | bytes 294912 | tf_op jit(solution)/shard_map/all_gather | solution.py:85
  263.8 1.1 multiply_reduce_fusion.3
  264.9 0.8 copy.41
  265.8 0.8 copy.35
  266.6 6.7 %fusion.12 = f32[512,8,64]{2,1,0:T(8,128)S(1)} fusion(f32[64]{0:T(128)S(1)} %iota_add_fusion, f32[16,512]{0,1:T(8,128)S(1)} %copy.29, f32[16,512]{0,1:T(8,128)} %copy-done.9, f32[8]{0:T(128)S(1)} %multiply_convert_fusion.3, f32[16,512]{0,1:T(8,128)} %copy.35), kind=kOutput, calls=%fused_computation.15 | convolution fusion | flops 51511296 | bytes 1147168 | tf_op jit(solution)/shard_map/nac,nkc->kac/dot_general | solution.py:51
  273.3 6.5 %add_bitcast_fusion.1 = f32[8,64,512]{1,0,2:T(8,128)} fusion(f32[512,8,64]{2,1,0:T(8,128)S(1)} %fusion.12, f32[512,8,64]{2,1,0:T(8,128)S(1)} %copy-done.8, f32[64]{0:T(128)S(1)} %iota_add_fusion, f32[16,512]{0,1:T(8,128)S(1)} %copy.29, f32[16,512]{0,1:T(8,128)S(1)} %copy-done.10, f32[16,9,512]{0,1,2:T(8,128)S(1)} %bitcast.55), kind=kOutput, calls=%fused_computation.45 | convolution fusion | flops 51904512 | bytes 7864832 | tf_op jit(solution)/shard_map/nac,nkc->kac/dot_general | solution.py:35
  279.8 3.2 copy.37
  283.0 6.5 %fusion.10 = f32[512,8,64]{2,1,0:T(8,128)S(1)} fusion(f32[64]{0:T(128)S(1)} %iota_add_fusion, f32[16,512]{0,1:T(8,128)S(1)} %copy.29, f32[16,512]{0,1:T(8,128)} %copy-done.9, f32[16,512]{0,1:T(8,128)} %copy.41, f32[8]{0:T(128)S(1)} %multiply_convert_fusion.3), kind=kOutput, calls=%fused_computation.13 | convolution fusion | flops 51511296 | bytes 1147168 | tf_op jit(solution)/shard_map/nac,nkc->kac/dot_general | solution.py:51
  289.5 6.5 %add_bitcast_fusion = f32[8,64,512]{1,0,2:T(8,128)} fusion(f32[512,8,64]{2,1,0:T(8,128)S(1)} %fusion.10, f32[512,8,64]{2,1,0:T(8,128)S(1)} %copy-done.7, f32[64]{0:T(128)S(1)} %iota_add_fusion, f32[16,512]{0,1:T(8,128)S(1)} %copy.29, f32[16,512]{0,1:T(8,128)S(1)} %copy-done.11, f32[16,9,512]{0,1,2:T(8,128)S(1)} %bitcast.53), kind=kOutput, calls=%fused_computation.43 | convolution fusion | flops 51904512 | bytes 7864832 | tf_op jit(solution)/shard_map/nac,nkc->kac/dot_general | solution.py:35
  296.0 3.2 copy.42
  299.2 8.9 %rev.7 = f32[512,512]{1,0:T(8,128)} reverse(f32[512,512]{1,0:T(8,128)} %bitcast.57), dimensions={0} | reverse | bytes 2097152 | tf_op jit(solution)/shard_map/rev | solution.py:102
  308.2 4.1 slice_multiply_fusion.5
  312.4 1.3 collective-permute-start.1
  313.7 1.8 collective-permute-done.1
  315.8 13.3 %fusion.8 = f32[512,4096]{1,0:T(8,128)} fusion(bf16[4096,512]{1,0:T(8,128)(2,1)} %get-tuple-element.10, bf16[4096,512]{1,0:T(8,128)(2,1)} %get-tuple-element.11, bf16[4096,512]{1,0:T(8,128)(2,1)} %get-tuple-element.9, f32[514,1536]{1,0:T(8,128)S(1)} %pad_maximum_fusion.3, f32[1536]{0:T(1024)S(1)} %get-tuple-element.8, f32[1536]{0:T(1024)S(1)} %get-tuple-element.7, ...), kind=kOutput, calls=%fused_computation.10 | convolution fusion | flops 6486491136 | bytes 30433280 | tf_op jit(solution)/shard_map/rk,dk->rd/dot_general | solution.py:117
  329.1 86.9 %reduce-scatter.2.cloned.1.call-done = f32[128,4096]{1,0:T(8,128)} async-done(((f32[512,4096]{1,0:T(8,128)}), f32[128,4096]{1,0:T(8,128)}) %reduce-scatter.2.cloned.1.call-update) | async-done | bytes 2097168 | tf_op jit(solution)/shard_map/reduce_scatter | solution.py:116
  416.0 2.7 convert_element_type.61
  (53 shorter events, 1.8 us)
Async XLA Ops:
  7.2 58.0 %all-gather.4.cloned.1.call-start = ((), (), s32[]{:S(2)}) async-start(), calls=%async_computation.1 | async-start | bytes 5242880 | tf_op jit(solution)/shard_map/all_gather | solution.py:59
  7.9 408.1 %reduce-scatter.2.cloned.1.call-start = ((), (), s32[]{:S(2)}) async-start(), calls=%async_computation.2 | async-start | bytes 10485760 | tf_op jit(solution)/shard_map/reduce_scatter | solution.py:116
  9.8 17.3 %copy-start.9 = (f32[16,512]{0,1:T(8,128)}, f32[16,512]{0,1:T(8,128)S(1)}, u32[]{:S(2)}) copy-start(f32[16,512]{0,1:T(8,128)S(1)} %copy.28) | copy-start | bytes 98308
  77.7 35.0 %collective-permute-start = (bf16[2,1536]{1,0:T(2,128)(2,1)S(1)}, bf16[2,1536]{1,0:T(2,128)(2,1)S(1)}, u32[]{:S(2)}, u32[]{:S(2)}) collective-permute-start(bf16[2,1536]{1,0:T(2,128)(2,1)S(1)} %slice.97), channel_id=1, source_target_pairs={{0,4},{4,8},{8,12},{12,16},{16,20},{20,24},{24,28},{1,5},{5,9},{9,... | collective-permute-start | bytes 18440 | tf_op jit(solution)/shard_map/ppermute | solution.py:12
  113.2 1.0 copy-start.12
  131.2 9.5 %copy-start.1 = (f32[8,64,512]{1,0,2:T(8,128)S(1)}, f32[8,64,512]{1,0,2:T(8,128)}, u32[]{:S(2)}) copy-start(f32[8,64,512]{1,0,2:T(8,128)} %copy.32) | copy-start | bytes 3145732
  140.7 30.2 %copy-start = (f32[8,64,512]{1,0,2:T(8,128)S(1)}, f32[8,64,512]{1,0,2:T(8,128)}, u32[]{:S(2)}) copy-start(f32[8,64,512]{1,0,2:T(8,128)} %copy.38) | copy-start | bytes 3145732
  266.6 6.7 %copy-start.3 = (f32[16,512,9]{0,2,1:T(8,128)S(1)}, f32[16,512,9]{0,2,1:T(8,128)}, u32[]{:S(2)}) copy-start(f32[16,512,9]{0,2,1:T(8,128)} %copy.50) | copy-start | bytes 884740
  266.6 6.7 %copy-start.8 = (f32[512,8,64]{2,1,0:T(8,128)S(1)}, f32[512,8,64]{2,1,0:T(8,128)}, u32[]{:S(2)}) copy-start(f32[512,8,64]{2,1,0:T(8,128)} %fusion.2) | copy-start | bytes 3145732
  266.6 6.7 %copy-start.10 = (f32[16,512]{0,1:T(8,128)S(1)}, f32[16,512]{0,1:T(8,128)}, u32[]{:S(2)}) copy-start(f32[16,512]{0,1:T(8,128)} %copy-done.9) | copy-start | bytes 98308
  283.0 6.5 %copy-start.2 = (f32[16,512,9]{0,2,1:T(8,128)S(1)}, f32[16,512,9]{0,2,1:T(8,128)}, u32[]{:S(2)}) copy-start(f32[16,512,9]{0,2,1:T(8,128)} %copy.58) | copy-start | bytes 884740
  283.0 6.5 %copy-start.7 = (f32[512,8,64]{2,1,0:T(8,128)S(1)}, f32[512,8,64]{2,1,0:T(8,128)}, u32[]{:S(2)}) copy-start(f32[512,8,64]{2,1,0:T(8,128)} %fusion) | copy-start | bytes 3145732
  283.0 6.5 %copy-start.11 = (f32[16,512]{0,1:T(8,128)S(1)}, f32[16,512]{0,1:T(8,128)}, u32[]{:S(2)}) copy-start(f32[16,512]{0,1:T(8,128)} %copy-done.9) | copy-start | bytes 98308
  296.0 12.1 %copy-start.13 = (f32[512]{0:T(512)S(1)}, f32[512]{0:T(512)}, u32[]{:S(2)}) copy-start(f32[512]{0:T(512)} %param.12) | copy-start | bytes 6148
  312.2 3.3 copy-start.4
  312.2 3.3 copy-start.5
  312.2 3.3 copy-start.6
  312.4 3.1 collective-permute-start.1
Sparse Core Ops, SparseCore 0:
  9.8 55.2 all-gather.3
  329.2 86.7 reduce-scatter.1
where the time goes:
time: 433 us; the launch traced here: 426 us
  matrix products  130 us (30%)
  waiting for transfers between devices  127 us (29%)
  local copies, waits for them, and re-layouts  100 us (23%)
  blocking collectives  28.9 us (7%)
  other arithmetic  21.2 us (5%)
  between operations  14.6 us (3%)
    reduce_scatter x1, waiting for transfers between devices, shards(): lax.psum_scatter(jnp.einsum('rk,dk->rd', grad_streams, weight_cat, prefer...  86.9 us
    dot_general x2, matrix products, modal_block(): jnp.einsum('abc,kbc->kac', toeplitz, sections, precision=exact_mode)  60.7 us
    all_gather x1, waiting for transfers between devices, shards(): lax.all_gather(tokens, 'tp', axis=0, tiled=True)  38 us
    gather x2, local copies, waits for them, and re-layouts, modal_block(): filter_taps[jnp.maximum(lag_index, 0)]  33.1 us
    dot_general x2, matrix products, modal_block(): jnp.einsum('nbc,kbc->nkc', to_end, sections, precision=exact_mode)  17.8 us
    all_gather x1, blocking collectives, shards(): lax.all_gather(backward_sum[None], 'ctx', axis=0, tiled=True)  14.7 us
    all_gather x1, blocking collectives, shards(): lax.all_gather(forward_sum[None], 'ctx', axis=0, tiled=True)  14.2 us
    dot_general x1, matrix products, shards(): jnp.einsum('rk,dk->rd', grad_streams, weight_cat, preferred_element_type=...  13.3 us
  transfers between devices with their start and end apart: 4, of which 3 were waited for; matrix products, arithmetic and copies ran while one was open for 12% of the time, Pallas kernels for 0%

commit v1 on v0

--- a/solution.py
+++ b/solution.py
@@ -56,7 +56,9 @@
     width = in_weight.shape[2]
     weight_cat = jnp.concatenate([in_weight[0], in_weight[1], in_weight[2]], axis=1)
     streams = jnp.dot(
-        lax.all_gather(tokens, "tp", axis=0, tiled=True),
+        jnp.concatenate(
+            lax.all_to_all(jnp.stack([tokens] * lax.axis_size("tp")), "tp", 0, 0), axis=0
+        ),
         weight_cat,
         preferred_element_type=jnp.float32,
     ).astype(jnp.bfloat16)

time: 433 us -> 433 us (level)
  waiting for transfers between devices: 127 us -> 122 us
  starting transfers between devices: 3.11 us -> 8.08 us
    all_gather x1 -> x0, waiting for transfers between devices: 38 us -> none  [shards(): lax.all_gather(tokens, 'tp', axis=0, tiled=True)]
    all_to_all x0 -> x1, waiting for transfers between devices: none -> 33 us  [shards(): lax.all_to_all(jnp.stack([tokens] * lax.axis_size('tp')), 'tp', 0, 0)]
    all_to_all x0 -> x1, starting transfers between devices: none -> 5.32 us  [shards(): lax.all_to_all(jnp.stack([tokens] * lax.axis_size('tp')), 'tp', 0, 0)]
  transfers between devices with their start and end apart: 4 -> 4, of which waited for: 3 -> 3; matrix products, arithmetic and copies ran while one was open for 12% -> 11% of each run, Pallas kernels for 0% -> 0%
where the time goes in v1:
time: 433 us; the launch traced here: 426 us
  matrix products  130 us (30%)
  waiting for transfers between devices  122 us (28%)
  local copies, waits for them, and re-layouts  101 us (23%)
  blocking collectives  29.6 us (7%)
  other arithmetic  20.5 us (5%)
  between operations  14.6 us (3%)
  starting transfers between devices  8.08 us (2%)
    reduce_scatter x1, waiting for transfers between devices, shards(): lax.psum_scatter(jnp.einsum('rk,dk->rd', grad_streams, weight_cat, prefer...  86.9 us
    dot_general x2, matrix products, modal_block(): jnp.einsum('abc,kbc->kac', toeplitz, sections, precision=exact_mode)  60.7 us
    gather x2, local copies, waits for them, and re-layouts, modal_block(): filter_taps[jnp.maximum(lag_index, 0)]  33.1 us
    all_to_all x1, waiting for transfers between devices, shards(): lax.all_to_all(jnp.stack([tokens] * lax.axis_size('tp')), 'tp', 0, 0)  33 us
    dot_general x2, matrix products, modal_block(): jnp.einsum('nbc,kbc->nkc', to_end, sections, precision=exact_mode)  17.8 us
    all_gather x1, blocking collectives, shards(): lax.all_gather(backward_sum[None], 'ctx', axis=0, tiled=True)  15.4 us
    all_gather x1, blocking collectives, shards(): lax.all_gather(forward_sum[None], 'ctx', axis=0, tiled=True)  14.2 us
    dot_general x1, matrix products, shards(): jnp.einsum('rk,dk->rd', grad_streams, weight_cat, preferred_element_type=...  13.3 us
  transfers between devices with their start and end apart: 4, of which 3 were waited for; matrix products, arithmetic and copies ran while one was open for 11% of the time, Pallas kernels for 0%

profile of v1, /device:TPU:0, one launch (start us, length us, event | category | flops | bytes accessed | tf_op | source)
XLA Modules:
  0.0 426.0 jit_solution(2319887598778068317)
XLA Ops:
  7.2 3.7 stack.2
  10.9 5.3 %all-to-all-start = ((bf16[4,128,4096]{2,1,0:T(8,128)(2,1)}), bf16[4,128,4096]{2,1,0:T(8,128)(2,1)}, u32[]{:S(2)}, u32[]{:S(2)}) async-start(bf16[4,128,4096]{2,1,0:T(8,128)(2,1)} %stack.2), calls=%async_computation | async-start | bytes 8388608 | tf_op jit(solution)/shard_map/all_to_all | solution.py:60
  16.9 6.0 %multiply_reduce_fusion = f32[64,512]{0,1:T(8,128)S(1)} fusion(f32[16,512]{0,1:T(8,128)S(1)} %copy.29, f32[16,512]{0,1:T(8,128)S(1)} %copy.28), kind=kLoop, calls=%fused_computation.20 | loop fusion | flops 1540096 | bytes 196608 | tf_op jit(solution)/shard_map/reduce_sum | solution.py:22
  22.8 9.0 %slice_bitcast_fusion.2 = (bf16[4096,512]{1,0:T(8,128)(2,1)}, bf16[4096,512]{1,0:T(8,128)(2,1)}, bf16[4096,512]{1,0:T(8,128)(2,1)}) fusion(bf16[3,4096,512]{2,1,0:T(8,128)(2,1)} %param.8), kind=kLoop, calls=%fused_computation.23 | loop fusion | bytes 25165824 | tf_op jit(solution)/shard_map/squeeze | solution.py:57
  31.9 33.0 %all-to-all-done = bf16[4,128,4096]{2,1,0:T(8,128)(2,1)} async-done(((bf16[4,128,4096]{2,1,0:T(8,128)(2,1)}), bf16[4,128,4096]{2,1,0:T(8,128)(2,1)}, u32[]{:S(2)}, u32[]{:S(2)}) %all-to-all-start) | async-done | bytes 4194336 | tf_op jit(solution)/shard_map/all_to_all | solution.py:60
  64.8 12.5 %fusion.22 = bf16[512,1536]{1,0:T(8,128)(2,1)S(1)} fusion(bf16[512,4096]{1,0:T(8,128)(2,1)} %bitcast.10, bf16[4096,512]{1,0:T(8,128)(2,1)} %get-tuple-element.10, bf16[4096,512]{1,0:T(8,128)(2,1)} %get-tuple-element.11, bf16[4096,512]{1,0:T(8,128)(2,1)} %get-tuple-element.9), kind=kOutput, calls=%fused_computation.37 | convolution fusion | flops 6480986112 | bytes 18350080 | tf_op jit(solution)/shard_map/dot_general | solution.py:58
  77.3 1.5 collective-permute-start
  78.9 16.8 %gather_fusion = f32[4096,512]{1,0:T(8,128)} fusion(f32[64,512]{1,0:T(8,128)S(1)} %copy.30, s32[4096]{0:T(1024)S(1)} %broadcast_clamp_fusion), kind=kCustom, calls=%fused_computation | custom fusion | bytes 16793600 | tf_op jit(solution)/shard_map/gather | solution.py:24
  95.7 16.3 %copy.31 = f32[64,64,512]{1,0,2:T(8,128)} copy(f32[64,64,512]{2,1,0:T(8,128)} %bitcast.52) | data formatting | bytes 16777216 | tf_op jit(solution)/shard_map/gather | solution.py:24
  112.1 0.5 maximum_convert_fusion
  112.6 0.9 fusion.19
  113.6 1.8 convert_multiply_fusion
  115.4 8.9 %rev.6 = f32[512,512]{1,0:T(8,128)} reverse(f32[512,512]{1,0:T(8,128)} %get-tuple-element.15), dimensions={0} | reverse | bytes 2097152 | tf_op jit(solution)/shard_map/rev | solution.py:84
  124.3 3.2 copy.38
  127.5 3.2 copy.32
  130.7 9.5 %fusion.43 = f32[16,512,8]{0,2,1:T(8,128)} fusion(f32[8,64,512]{1,0,2:T(8,128)} %copy.32, f32[64]{0:T(128)S(1)} %iota_subtract_fusion.2, f32[16,512]{0,1:T(8,128)S(1)} %copy.29), kind=kOutput, calls=%fused_computation.64 | convolution fusion | flops 50855936 | bytes 1343744 | tf_op jit(solution)/shard_map/nbc,kbc->nkc/dot_general | solution.py:27
  140.1 30.2 %fusion.2 = f32[512,8,64]{2,1,0:T(8,128)} fusion(f32[8,64,512]{1,0,2:T(8,128)S(1)} %copy-done.1, f32[64,64,512]{1,0,2:T(8,128)} %copy.31, pred[64,64]{1,0:T(8,128)(4,1)S(1)} %subtract_compare_fusion), kind=kOutput, calls=%fused_computation.3 | convolution fusion | flops 203423744 | bytes 10489856 | tf_op jit(solution)/shard_map/abc,kbc->kac/dot_general | solution.py:25
  170.3 30.5 %fusion = f32[512,8,64]{2,1,0:T(8,128)} fusion(f32[8,64,512]{1,0,2:T(8,128)S(1)} %copy-done, f32[64,64,512]{1,0,2:T(8,128)} %copy.31, pred[64,64]{1,0:T(8,128)(4,1)S(1)} %subtract_compare_fusion), kind=kOutput, calls=%fused_computation.1 | convolution fusion | flops 203423744 | bytes 10489856 | tf_op jit(solution)/shard_map/abc,kbc->kac/dot_general | solution.py:25
  200.9 8.3 %fusion.44 = f32[16,512,8]{0,2,1:T(8,128)} fusion(f32[8,64,512]{1,0,2:T(8,128)S(1)} %copy-done, f32[64]{0:T(128)S(1)} %iota_subtract_fusion.2, f32[16,512]{0,1:T(8,128)S(1)} %copy.29), kind=kOutput, calls=%fused_computation.65 | convolution fusion | flops 50855936 | bytes 1343744 | tf_op jit(solution)/shard_map/nbc,kbc->nkc/dot_general | solution.py:27
  209.2 2.9 copy.61
  212.0 2.9 copy.62
  214.9 2.8 multiply_reduce_fusion.1
  217.7 4.5 %copy.58 = f32[16,512,9]{0,2,1:T(8,128)} copy(f32[16,512,9]{1,0,2:T(8,128)} %get-tuple-element.2) | data formatting | bytes 589824 | tf_op jit(solution)/shard_map/kmnc,nmc->nkc/dot_general | solution.py:33
  222.2 2.4 slice.107
  224.6 1.0 copy.40
  225.7 15.4 %all-gather.1 = f32[128,1,512]{2,1,0:T(1,128)S(1)} all-gather(f32[16,1,512]{2,1,0:T(1,128)S(1)} %copy.40), channel_id=3, replica_groups=mesh['ctx'=8,'tp'=4] {'ctx'}, dimensions={0}, use_global_device_ids=true | all-gather | bytes 294912 | tf_op jit(solution)/shard_map/all_gather | solution.py:88
  241.1 0.7 copy.60
  241.8 4.5 %copy.50 = f32[16,512,9]{0,2,1:T(8,128)} copy(f32[16,512,9]{1,0,2:T(8,128)} %get-tuple-element.3) | data formatting | bytes 589824 | tf_op jit(solution)/shard_map/kmnc,nmc->nkc/dot_general | solution.py:33
  246.3 2.4 slice.105
  248.8 1.0 copy.34
  249.8 14.2 %all-gather = f32[128,1,512]{2,1,0:T(1,128)S(1)} all-gather(f32[16,1,512]{2,1,0:T(1,128)S(1)} %copy.34), channel_id=2, replica_groups=mesh['ctx'=8,'tp'=4] {'ctx'}, dimensions={0}, use_global_device_ids=true | all-gather | bytes 294912 | tf_op jit(solution)/shard_map/all_gather | solution.py:87
  264.0 1.1 multiply_reduce_fusion.3
  265.2 0.8 copy.41
  266.0 0.8 copy.35
  266.9 6.7 %fusion.12 = f32[512,8,64]{2,1,0:T(8,128)S(1)} fusion(f32[64]{0:T(128)S(1)} %iota_add_fusion, f32[16,512]{0,1:T(8,128)S(1)} %copy.29, f32[16,512]{0,1:T(8,128)} %copy-done.9, f32[8]{0:T(128)S(1)} %multiply_convert_fusion.3, f32[16,512]{0,1:T(8,128)} %copy.35), kind=kOutput, calls=%fused_computation.15 | convolution fusion | flops 51511296 | bytes 1147168 | tf_op jit(solution)/shard_map/nac,nkc->kac/dot_general | solution.py:51
  273.6 6.5 %add_bitcast_fusion.1 = f32[8,64,512]{1,0,2:T(8,128)} fusion(f32[512,8,64]{2,1,0:T(8,128)S(1)} %fusion.12, f32[512,8,64]{2,1,0:T(8,128)S(1)} %copy-done.8, f32[64]{0:T(128)S(1)} %iota_add_fusion, f32[16,512]{0,1:T(8,128)S(1)} %copy.29, f32[16,512]{0,1:T(8,128)S(1)} %copy-done.10, f32[16,9,512]{0,1,2:T(8,128)S(1)} %bitcast.56), kind=kOutput, calls=%fused_computation.45 | convolution fusion | flops 51904512 | bytes 7864832 | tf_op jit(solution)/shard_map/nac,nkc->kac/dot_general | solution.py:35
  280.1 3.2 copy.37
  283.2 6.5 %fusion.10 = f32[512,8,64]{2,1,0:T(8,128)S(1)} fusion(f32[64]{0:T(128)S(1)} %iota_add_fusion, f32[16,512]{0,1:T(8,128)S(1)} %copy.29, f32[16,512]{0,1:T(8,128)} %copy-done.9, f32[16,512]{0,1:T(8,128)} %copy.41, f32[8]{0:T(128)S(1)} %multiply_convert_fusion.3), kind=kOutput, calls=%fused_computation.13 | convolution fusion | flops 51511296 | bytes 1147168 | tf_op jit(solution)/shard_map/nac,nkc->kac/dot_general | solution.py:51
  289.8 6.5 %add_bitcast_fusion = f32[8,64,512]{1,0,2:T(8,128)} fusion(f32[512,8,64]{2,1,0:T(8,128)S(1)} %fusion.10, f32[512,8,64]{2,1,0:T(8,128)S(1)} %copy-done.7, f32[64]{0:T(128)S(1)} %iota_add_fusion, f32[16,512]{0,1:T(8,128)S(1)} %copy.29, f32[16,512]{0,1:T(8,128)S(1)} %copy-done.11, f32[16,9,512]{0,1,2:T(8,128)S(1)} %bitcast.54), kind=kOutput, calls=%fused_computation.43 | convolution fusion | flops 51904512 | bytes 7864832 | tf_op jit(solution)/shard_map/nac,nkc->kac/dot_general | solution.py:35
  296.3 3.2 copy.42
  299.5 8.9 %rev.7 = f32[512,512]{1,0:T(8,128)} reverse(f32[512,512]{1,0:T(8,128)} %bitcast.58), dimensions={0} | reverse | bytes 2097152 | tf_op jit(solution)/shard_map/rev | solution.py:104
  308.4 4.1 slice_multiply_fusion.5
  312.7 1.3 collective-permute-start.1
  314.0 1.8 collective-permute-done.1
  315.8 0.2 pad_maximum_fusion.3
  316.0 13.3 %fusion.8 = f32[512,4096]{1,0:T(8,128)} fusion(bf16[4096,512]{1,0:T(8,128)(2,1)} %get-tuple-element.10, bf16[4096,512]{1,0:T(8,128)(2,1)} %get-tuple-element.11, bf16[4096,512]{1,0:T(8,128)(2,1)} %get-tuple-element.9, f32[514,1536]{1,0:T(8,128)S(1)} %pad_maximum_fusion.3, f32[1536]{0:T(1024)S(1)} %get-tuple-element.8, f32[1536]{0:T(1024)S(1)} %get-tuple-element.7, ...), kind=kOutput, calls=%fused_computation.10 | convolution fusion | flops 6486491136 | bytes 30433280 | tf_op jit(solution)/shard_map/rk,dk->rd/dot_general | solution.py:119
  329.3 86.9 %reduce-scatter.2.cloned.1.call-done = f32[128,4096]{1,0:T(8,128)} async-done(((f32[512,4096]{1,0:T(8,128)}), f32[128,4096]{1,0:T(8,128)}) %reduce-scatter.2.cloned.1.call-update) | async-done | bytes 2097168 | tf_op jit(solution)/shard_map/reduce_scatter | solution.py:118
  416.3 2.7 convert_element_type.61
  (59 shorter events, 1.1 us)
Async XLA Ops:
  10.9 5.4 %copy-start.14 = (f32[16,512]{1,0:T(8,128)S(1)}, f32[16,512]{1,0:T(8,128)}, u32[]{:S(2)}) copy-start(f32[16,512]{1,0:T(8,128)} %param.10) | copy-start | bytes 98308
  10.9 5.6 %copy-start.13 = (f32[16,512]{1,0:T(8,128)S(1)}, f32[16,512]{1,0:T(8,128)}, u32[]{:S(2)}) copy-start(f32[16,512]{1,0:T(8,128)} %param.11) | copy-start | bytes 98308
  10.9 6.0 %copy-start.15 = (f32[3,3,512]{2,1,0:T(4,128)S(1)}, f32[3,3,512]{2,1,0:T(4,128)}, u32[]{:S(2)}) copy-start(f32[3,3,512]{2,1,0:T(4,128)} %param.9) | copy-start | bytes 55300
  10.9 54.0 %all-to-all-start = ((bf16[4,128,4096]{2,1,0:T(8,128)(2,1)}), bf16[4,128,4096]{2,1,0:T(8,128)(2,1)}, u32[]{:S(2)}, u32[]{:S(2)}) async-start(bf16[4,128,4096]{2,1,0:T(8,128)(2,1)} %stack.2), calls=%async_computation | async-start | bytes 8388608 | tf_op jit(solution)/shard_map/all_to_all | solution.py:60
  16.2 400.1 %reduce-scatter.2.cloned.1.call-start = ((), (), s32[]{:S(2)}) async-start(), calls=%async_computation.2 | async-start | bytes 10485760 | tf_op jit(solution)/shard_map/reduce_scatter | solution.py:118
  16.6 15.3 %copy-start.9 = (f32[16,512]{0,1:T(8,128)}, f32[16,512]{0,1:T(8,128)S(1)}, u32[]{:S(2)}) copy-start(f32[16,512]{0,1:T(8,128)S(1)} %copy.28) | copy-start | bytes 98308
  77.3 34.7 %collective-permute-start = (bf16[2,1536]{1,0:T(2,128)(2,1)S(1)}, bf16[2,1536]{1,0:T(2,128)(2,1)S(1)}, u32[]{:S(2)}, u32[]{:S(2)}) collective-permute-start(bf16[2,1536]{1,0:T(2,128)(2,1)S(1)} %slice.97), channel_id=1, source_target_pairs={{0,4},{4,8},{8,12},{12,16},{16,20},{20,24},{24,28},{1,5},{5,9},{9,... | collective-permute-start | bytes 18440 | tf_op jit(solution)/shard_map/ppermute | solution.py:12
  112.6 1.0 copy-start.12
  130.7 9.5 %copy-start.1 = (f32[8,64,512]{1,0,2:T(8,128)S(1)}, f32[8,64,512]{1,0,2:T(8,128)}, u32[]{:S(2)}) copy-start(f32[8,64,512]{1,0,2:T(8,128)} %copy.32) | copy-start | bytes 3145732
  140.1 30.2 %copy-start = (f32[8,64,512]{1,0,2:T(8,128)S(1)}, f32[8,64,512]{1,0,2:T(8,128)}, u32[]{:S(2)}) copy-start(f32[8,64,512]{1,0,2:T(8,128)} %copy.38) | copy-start | bytes 3145732
  266.9 6.7 %copy-start.3 = (f32[16,512,9]{0,2,1:T(8,128)S(1)}, f32[16,512,9]{0,2,1:T(8,128)}, u32[]{:S(2)}) copy-start(f32[16,512,9]{0,2,1:T(8,128)} %copy.50) | copy-start | bytes 884740
  266.9 6.7 %copy-start.8 = (f32[512,8,64]{2,1,0:T(8,128)S(1)}, f32[512,8,64]{2,1,0:T(8,128)}, u32[]{:S(2)}) copy-start(f32[512,8,64]{2,1,0:T(8,128)} %fusion.2) | copy-start | bytes 3145732
  266.9 6.7 %copy-start.10 = (f32[16,512]{0,1:T(8,128)S(1)}, f32[16,512]{0,1:T(8,128)}, u32[]{:S(2)}) copy-start(f32[16,512]{0,1:T(8,128)} %copy-done.9) | copy-start | bytes 98308
  283.2 6.5 %copy-start.2 = (f32[16,512,9]{0,2,1:T(8,128)S(1)}, f32[16,512,9]{0,2,1:T(8,128)}, u32[]{:S(2)}) copy-start(f32[16,512,9]{0,2,1:T(8,128)} %copy.58) | copy-start | bytes 884740
  283.2 6.5 %copy-start.7 = (f32[512,8,64]{2,1,0:T(8,128)S(1)}, f32[512,8,64]{2,1,0:T(8,128)}, u32[]{:S(2)}) copy-start(f32[512,8,64]{2,1,0:T(8,128)} %fusion) | copy-start | bytes 3145732
  283.2 6.5 %copy-start.11 = (f32[16,512]{0,1:T(8,128)S(1)}, f32[16,512]{0,1:T(8,128)}, u32[]{:S(2)}) copy-start(f32[16,512]{0,1:T(8,128)} %copy-done.9) | copy-start | bytes 98308
  296.3 12.1 %copy-start.16 = (f32[512]{0:T(512)S(1)}, f32[512]{0:T(512)}, u32[]{:S(2)}) copy-start(f32[512]{0:T(512)} %param.12) | copy-start | bytes 6148
  312.5 3.3 copy-start.4
  312.5 3.3 copy-start.5
  312.5 3.3 copy-start.6
  312.7 3.1 collective-permute-start.1
Sparse Core Ops, SparseCore 0:
  329.4 86.7 reduce-scatter.1
